TPU v7x, 32 devices: a whole 2x2x4 slice. The times are simulated.
32 devices in a mesh: gx: 4 (over z), yz: 8 (over y, x, core).
Axes of the slice: x: 2, y: 2, z: 4, core: 2. Of those that a mesh axis runs over, the one named last changes fastest.
Arguments:
- fields: float32 [5, 64, 2048], P(None, 'gx', 'yz'), may hold values from -6 to 6
- ghost_target: int32 [4, 512], P('gx', 'yz'), may hold values from 0 to 4095, as said below
- ghost_owner: int32 [4, 512, 1], P('gx', 'yz'), may hold values from 0 to 7; in each aligned block of 64 rows (0 to 63, 64 to 127, ..., all dimensions but the last counted through in order) at most 32 rows name the same one
- source_x: int32 [4, 512], P('gx', 'yz'), may hold values from 0 to 12
- source_col: int32 [4, 512], P('gx', 'yz'), may hold values from 0 to 255
- image_weights: float32 [4, 4, 512], P(None, 'gx', 'yz'), may hold values from 0 to 0.5
- sensor_bins: int32 [64, 2048], P('gx', 'yz'), may hold values from 0 to 7
Outputs:
- derivative: float32 [5, 64, 2048], P(None, 'gx', 'yz')
- filtered: float32 [5, 64, 2048], P(None, 'gx', 'yz')
Inputs may be any that keep to these rules, and one draw needn't show every extreme that they name: `ghost_target`: the 64 target cells of one device are distinct. `ghost_owner`: within the 64 entries of one device no owner is named more than 32 times.
All inputs are finite; a program needn't handle non-finite values.
Results may differ from a plain program's by a relative error of at most 0.00002.
Values sent between devices are 32-bit elements; how exact they have to be, the bound alone decides.
A program may use at most 64 MiB of HBM per device.

v0:
```python
import jax
import jax.numpy as jnp
from jax import lax
from jax.sharding import PartitionSpec as P

SIGNS = (1.0, -1.0, 1.0, 1.0, 1.0)
ALPHA_TOP = 0.499
ALPHA_STEP = 0.006


def with_halo(x, sides, width):
    for axis, dim in sides:
        count, length = (lax.axis_size(axis), x.shape[dim])
        up = [(i, (i + 1) % count) for i in range(count - 1)]
        down = [(j, i) for i, j in up]
        last = lax.slice_in_dim(x, length - width, length, axis=dim)
        leading = lax.slice_in_dim(x, 0, width, axis=dim)
        before = lax.ppermute(last, axis, up)
        after = lax.ppermute(leading, axis, down)
        x = jnp.concatenate([before, x, after], axis=dim)
    return x


def filter_weights(alpha):
    twice = 2.0 * alpha - 1.0
    return (
        (193.0 + 126.0 * alpha) / 256.0,
        (105.0 + 302.0 * alpha) / 256.0,
        15.0 * twice / 64.0,
        -45.0 * twice / 512.0,
        5.0 * twice / 256.0,
        -twice / 512.0,
    )


def stencils(padded, alpha, length):

    def plane(offset):
        return lax.slice_in_dim(padded, 5 + offset, 5 + offset + length, axis=1)

    slope = 7.0 / 9.0 * (plane(1) - plane(-1)) + 1.0 / 36.0 * (plane(2) - plane(-2))
    weights = filter_weights(alpha)
    smooth = weights[0] * plane(0)
    for offset in range(1, 6):
        smooth = smooth + 0.5 * weights[offset] * (plane(offset) + plane(-offset))
    return (slope, smooth)


def from_below(value, stride, fill):
    length = value.shape[-2]
    edge = jnp.full_like(lax.slice_in_dim(value, 0, stride, axis=value.ndim - 2), fill)
    return jnp.concatenate(
        [edge, lax.slice_in_dim(value, 0, length - stride, axis=value.ndim - 2)], axis=-2
    )


def from_above(value, stride, fill):
    length = value.shape[-2]
    edge = jnp.full_like(lax.slice_in_dim(value, 0, stride, axis=value.ndim - 2), fill)
    return jnp.concatenate(
        [lax.slice_in_dim(value, stride, length, axis=value.ndim - 2), edge], axis=-2
    )


def reduce_solve(coupling, right):
    length = coupling.shape[-2]
    lower = coupling.at[..., 0, :].set(0.0)
    upper = coupling.at[..., length - 1, :].set(0.0)
    middle = jnp.ones_like(coupling)
    stride = 1
    while stride < length:
        lower_m = from_below(lower, stride, 0.0)
        middle_m = from_below(middle, stride, 1.0)
        upper_m = from_below(upper, stride, 0.0)
        right_m = from_below(right, stride, 0.0)
        lower_p = from_above(lower, stride, 0.0)
        middle_p = from_above(middle, stride, 1.0)
        upper_p = from_above(upper, stride, 0.0)
        right_p = from_above(right, stride, 0.0)
        first_k = lower / middle_m
        second_k = upper / middle_p
        middle = middle - first_k * upper_m - second_k * lower_p
        right = right - first_k * right_m - second_k * right_p
        lower = -first_k * lower_m
        upper = -second_k * upper_p
        stride = stride * 2
    return right / middle


def interface_solve(right, coupling):
    cell_total = right.shape[1]
    left_unit = jnp.zeros_like(right).at[:, 0, :].set(-coupling[:, 0, :])
    right_unit = jnp.zeros_like(right).at[:, cell_total - 1, :].set(-coupling[:, cell_total - 1, :])
    solved = reduce_solve(coupling, jnp.stack([right, left_unit, right_unit], axis=0))
    edges = jnp.concatenate([solved[:, :, 0, :], solved[:, :, cell_total - 1, :]], axis=0)
    gathered = lax.all_gather(edges[None], "gx", axis=0, tiled=True)

    def forward(carry, item):
        hold_last, gain_last = carry
        scale = 1.0 - item[1] * gain_last
        hold_first = (item[0] + item[1] * hold_last) / scale
        gain_first = item[2] / scale
        new_hold = item[3] + item[4] * hold_last + item[4] * gain_last * hold_first
        new_gain = item[5] + item[4] * gain_last * gain_first
        return ((new_hold, new_gain), (hold_first, gain_first, new_hold, new_gain))

    zero = jnp.zeros(gathered.shape[2:], jnp.float32)
    unused, (hold_first, gain_first, hold_all, gain_all) = lax.scan(forward, (zero, zero), gathered)

    def backward(following, item):
        first = item[0] + item[1] * following
        return (first, first)

    unused_last, firsts = lax.scan(backward, zero, (hold_first, gain_first), reverse=True)
    rank_count = gathered.shape[0]
    own = lax.axis_index("gx")
    after = lax.dynamic_index_in_dim(
        firsts, jnp.minimum(own + 1, rank_count - 1), 0, keepdims=False
    )
    after = jnp.where(own < rank_count - 1, after, 0.0)
    before_index = jnp.maximum(own - 1, 0)
    own_first = lax.dynamic_index_in_dim(firsts, own, 0, keepdims=False)
    before = (
        lax.dynamic_index_in_dim(hold_all, before_index, 0, keepdims=False)
        + lax.dynamic_index_in_dim(gain_all, before_index, 0, keepdims=False) * own_first
    )
    before = jnp.where(own > 0, before, 0.0)
    return solved[0] + before[:, None, :] * solved[1] + after[:, None, :] * solved[2]


def shards(fields, ghost_target, ghost_owner, source_x, source_col, image_weights, sensor_bins):
    field_count, cell_count, column_count = fields.shape
    ghost_count = ghost_target.shape[1]
    yz_ranks = lax.axis_size("yz")
    capacity = 4 * (ghost_count // yz_ranks)
    owner = ghost_owner[0, :, 0]
    targets = ghost_target[0]
    member = (owner[:, None] == jnp.arange(yz_ranks, dtype=jnp.int32)[None, :]).astype(jnp.int32)
    slot = jnp.sum(jnp.cumsum(member, axis=0) * member, axis=1) - 1
    flat_source = (source_x[0] * column_count + source_col[0]).astype(jnp.float32)
    payload = jnp.zeros((5, yz_ranks, capacity), jnp.float32)
    payload = payload.at[0, owner, slot].set(flat_source)
    payload = payload.at[1:, owner, slot].set(image_weights[:, 0, :])
    flat_fields = fields.reshape(field_count, cell_count * column_count)
    requests = lax.all_to_all(payload, "yz", split_axis=1, concat_axis=1, tiled=True)
    position = requests[0].astype(jnp.int32)
    total = jnp.zeros((field_count,) + position.shape, jnp.float32)
    for offset in range(4):
        total = total + requests[1 + offset][None] * jnp.take(
            flat_fields, position + offset * column_count, axis=1
        )
    answers = lax.all_to_all(total, "yz", split_axis=1, concat_axis=1, tiled=True)
    values = answers[:, owner, slot] * jnp.array(SIGNS, jnp.float32)[:, None]
    filled = flat_fields.at[:, targets].set(values).reshape(fields.shape)
    padded = with_halo(filled, (("gx", 1),), 5)
    alpha = ALPHA_TOP - ALPHA_STEP * sensor_bins.astype(jnp.float32)
    slope, smooth = stencils(padded, alpha, cell_count)
    right = jnp.concatenate([slope, smooth], axis=0)
    coupling = jnp.concatenate(
        [jnp.full(slope.shape, 1.0 / 3.0, jnp.float32), jnp.broadcast_to(alpha, smooth.shape)],
        axis=0,
    )
    result = interface_solve(right, coupling)
    return (result[:field_count], result[field_count:])


def solution(mesh):
    placed = (
        P(None, "gx", "yz"),
        P("gx", "yz"),
        P("gx", "yz", None),
        P("gx", "yz"),
        P("gx", "yz"),
        P(None, "gx", "yz"),
        P("gx", "yz"),
    )
    return jax.shard_map(
        shards,
        mesh=mesh,
        in_specs=placed,
        out_specs=(P(None, "gx", "yz"), P(None, "gx", "yz")),
        check_vma=False,
    )
```

profile of v0, /device:TPU:0, one launch (start us, length us, event | category | flops | bytes accessed | tf_op | source)
XLA Modules:
  0.0 633.5 jit_solution(3069269054238274228)
XLA Ops:
  4.1 4.4 scatter_fusion
  9.5 564.5 %while.43 = (s32[]{:T(128)}, f32[5,8,32]{0,2,1:T(8,128)S(1)}, s32[64,3]{0,1:T(4,128)S(1)}, f32[64,4]{1,0:T(8,128)S(1)}, s32[]{:T(128)}, /*index=5*/s32[3]{0:T(128)}) while((s32[]{:T(128)}, f32[5,8,32]{0,2,1:T(8,128)S(1)}, s32[64,3]{0,1:T(4,128)S(1)}, f32[64,4]{1,0:T(8,128)S(1)}, s32[]{:T(128)}, /*index=5*/s32[3]{0:T(128)}) %tuple.171), condition=%wide.while_cond.4, body=%wide.while_body.4.sunk | while | flops 23 | bytes 255 | solution.py:143
  10.2 3.3 and_reduce_fusion.2
  19.0 3.3 and_reduce_fusion.2
  27.9 3.3 and_reduce_fusion.2
  36.7 3.3 and_reduce_fusion.2
  45.5 3.3 and_reduce_fusion.2
  54.3 3.3 and_reduce_fusion.2
  63.1 3.3 and_reduce_fusion.2
  72.0 3.3 and_reduce_fusion.2
  80.8 3.3 and_reduce_fusion.2
  89.6 3.3 and_reduce_fusion.2
  98.4 3.3 and_reduce_fusion.2
  107.2 3.3 and_reduce_fusion.2
  116.1 3.3 and_reduce_fusion.2
  124.9 3.3 and_reduce_fusion.2
  133.7 3.3 and_reduce_fusion.2
  142.5 3.3 and_reduce_fusion.2
  151.3 3.3 and_reduce_fusion.2
  160.2 3.3 and_reduce_fusion.2
  169.0 3.3 and_reduce_fusion.2
  177.8 3.3 and_reduce_fusion.2
  186.6 3.3 and_reduce_fusion.2
  195.4 3.3 and_reduce_fusion.2
  204.3 3.3 and_reduce_fusion.2
  213.1 3.3 and_reduce_fusion.2
  221.9 3.3 and_reduce_fusion.2
  230.7 3.3 and_reduce_fusion.2
  239.5 3.3 and_reduce_fusion.2
  248.4 3.3 and_reduce_fusion.2
  257.2 3.3 and_reduce_fusion.2
  266.0 3.3 and_reduce_fusion.2
  274.8 3.3 and_reduce_fusion.2
  283.6 3.3 and_reduce_fusion.2
  292.5 3.3 and_reduce_fusion.2
  301.3 3.3 and_reduce_fusion.2
  310.1 3.3 and_reduce_fusion.2
  318.9 3.3 and_reduce_fusion.2
  327.7 3.3 and_reduce_fusion.2
  336.6 3.3 and_reduce_fusion.2
  345.4 3.3 and_reduce_fusion.2
  354.2 3.3 and_reduce_fusion.2
  363.0 3.3 and_reduce_fusion.2
  574.8 5.2 all-to-all-start
  595.5 3.4 all-to-all-start.1
  600.0 3.5 all-to-all-done.1
  608.5 4.5 collective-permute-start.1
  616.9 15.4 %all-gather = f32[24,10,256]{2,1,0:T(8,128)S(1)} all-gather(f32[6,10,256]{2,1,0:T(8,128)S(1)} %copy.89), channel_id=2, replica_groups=mesh['gx'=4,'yz'=8] {'gx'}, dimensions={0}, use_global_device_ids=true | all-gather | bytes 307200 | tf_op jit(solution)/shard_map/all_gather | solution.py:96
  (406 shorter events, 459.7 us)
Async XLA Ops:
  574.8 9.9 %all-to-all-start = ((f32[8,1,160]{2,1,0:T(1,128)}), f32[8,1,160]{2,1,0:T(1,128)S(1)}, u32[]{:S(2)}, u32[]{:S(2)}) async-start(f32[8,1,160]{2,1,0:T(1,128)} %reshape.400), calls=%async_computation | async-start | bytes 16384 | tf_op jit(solution)/shard_map/all_to_all | solution.py:145
  582.2 1.0 copy-start.2
  595.5 8.1 %all-to-all-start.1 = ((f32[8,1,160]{2,1,0:T(1,128)}), f32[8,1,160]{2,1,0:T(1,128)S(1)}, u32[]{:S(2)}, u32[]{:S(2)}) async-start(f32[8,1,160]{2,1,0:T(1,128)} %reshape.402), calls=%async_computation.1 | async-start | bytes 16384 | tf_op jit(solution)/shard_map/all_to_all | solution.py:152
  604.4 10.3 %copy-start.3 = (f32[16,256]{1,0:T(8,128)S(1)}, f32[16,256]{1,0:T(8,128)}, u32[]{:S(2)}) copy-start(f32[16,256]{1,0:T(8,128)} %get-tuple-element.417) | copy-start | bytes 49156
  604.4 10.3 %copy-start.4 = (f32[16,256]{1,0:T(8,128)S(1)}, f32[16,256]{1,0:T(8,128)}, u32[]{:S(2)}) copy-start(f32[16,256]{1,0:T(8,128)} %get-tuple-element.418) | copy-start | bytes 49156
  604.4 10.3 %copy-start.5 = (f32[16,256]{1,0:T(8,128)S(1)}, f32[16,256]{1,0:T(8,128)}, u32[]{:S(2)}) copy-start(f32[16,256]{1,0:T(8,128)} %get-tuple-element.419) | copy-start | bytes 49156
  604.4 10.3 %copy-start.6 = (f32[16,256]{1,0:T(8,128)S(1)}, f32[16,256]{1,0:T(8,128)}, u32[]{:S(2)}) copy-start(f32[16,256]{1,0:T(8,128)} %get-tuple-element.420) | copy-start | bytes 49156
  606.5 8.2 %copy-start.7 = (f32[16,256]{1,0:T(8,128)S(1)}, f32[16,256]{1,0:T(8,128)}, u32[]{:S(2)}) copy-start(f32[16,256]{1,0:T(8,128)} %get-tuple-element.421) | copy-start | bytes 49156
  607.2 5.9 collective-permute-start
  608.5 6.2 collective-permute-start.1
  615.6 0.9 copy-start
  615.6 1.0 copy-start.1
where the time goes:
time: 641 us; the launch traced here: 634 us
  other arithmetic  391 us (61%)
  local copies, waits for them, and re-layouts  204 us (32%)
  blocking collectives  15.4 us (2%)
  starting transfers between devices  14.4 us (2%)
    scatter x128, other arithmetic  377 us
    scatter x192, local copies, waits for them, and re-layouts  186 us
    all_gather x1, blocking collectives, interface_solve(): gathered = lax.all_gather(edges[None], 'gx', axis=0, tiled=True)  15.4 us
  transfers between devices with their start and end apart: 4, of which 3 were waited for; matrix products, arithmetic and copies ran while one was open for 1% of the time, Pallas kernels for 0%

commit v1 on v0

v1 whole, which is shorter than its diff:
```python
import functools

import jax
import jax.numpy as jnp
from jax import lax
from jax.experimental import pallas as pl
from jax.experimental.pallas import tpu as pltpu
from jax.sharding import PartitionSpec as P

MESH = pl.DeviceIdType.MESH
SIGNS = (1.0, -1.0, 1.0, 1.0, 1.0)
ALPHA_TOP = 0.499
ALPHA_STEP = 0.006
HALO = 5
ROWS = 8


def thirds_factors(cells):
    a = 1.0 / 3.0
    link, inverse, last = ([], [], 0.0)
    for x in range(cells):
        inv = 1.0 / (1.0 - (a * last if x else 0.0))
        last = a * inv
        inverse.append(inv)
        link.append(last)
    left, right = ([0.0] * cells, [0.0] * cells)
    y = -link[0]
    left[0] = y
    for x in range(1, cells):
        y = -link[x] * y
        left[x] = y
    right[-1] = -link[-1]
    for x in range(cells - 2, -1, -1):
        left[x] = left[x] - link[x] * left[x + 1]
        right[x] = -link[x] * right[x + 1]
    return (link, inverse, left, right)


def thirds_interface(ranks, left, right):
    l0, l1, r0, r1 = (left[0], left[-1], right[0], right[-1])
    gain, out = (0.0, [])
    for q in range(ranks):
        s = 1.0 / (1.0 - l0 * gain)
        gf = r0 * s
        ng = r1 + l1 * gain * gf
        out.append((s, l0 * s, gf, l1, l1 * gain, ng))
        gain = ng
    return out


def split3(v):
    hi = v.astype(jnp.bfloat16)
    rest = v - hi.astype(jnp.float32)
    mid = rest.astype(jnp.bfloat16)
    low = (rest - mid.astype(jnp.float32)).astype(jnp.bfloat16)
    return (hi, mid, low)


def kernel(
    n_gx,
    n_yz,
    fields,
    target,
    owner,
    sx,
    col,
    weights,
    sensor,
    out_d,
    out_g,
    parts,
    onehot_t,
    reqs,
    reps,
    answers,
    fb,
    coef,
    gains,
    edges,
    unit_d,
    unit_g,
    sol,
    pick,
    req_s,
    req_r,
    rep_s,
    rep_r,
    gain_s,
    gain_r,
    halo_s,
    halo_r,
    edge_s,
    edge_r,
):
    F, X, C = fields.shape
    G = target.shape[1]
    GP = reqs.shape[2]
    pack = GP // G
    p = lax.axis_index("gx")
    r = lax.axis_index("yz")
    f32, bf16 = (jnp.float32, jnp.bfloat16)

    def yz(k):
        return (p, lax.rem(r + k + n_yz, n_yz))

    def gx(k):
        return (lax.rem(p + k + n_gx, n_gx), r)

    barrier = pltpu.get_barrier_semaphore()
    fb[...] = jnp.zeros_like(fb)
    edges[...] = jnp.zeros_like(edges)
    for k in range(1, n_yz):
        pl.semaphore_signal(barrier, inc=1, device_id=yz(k), device_id_type=MESH)
    for k in range(1, n_gx):
        pl.semaphore_signal(barrier, inc=1, device_id=gx(k), device_id_type=MESH)

    reqs[0] = jnp.zeros((ROWS, GP), f32)
    reqs[0, 0:1, 0:G] = col[...].astype(f32)
    reqs[0, 1:2, 0:G] = sx[...].astype(f32)
    reqs[0, 2:3, 0:G] = owner[...].astype(f32)
    for k in range(4):
        reqs[0, 3 + k : 4 + k, 0:G] = weights[k]

    pl.semaphore_wait(barrier, n_yz - 1 + n_gx - 1)

    def req_copy(k):
        return pltpu.make_async_remote_copy(
            src_ref=reqs.at[0],
            dst_ref=reqs.at[k],
            send_sem=req_s.at[k],
            recv_sem=req_r.at[k],
            device_id=yz(k),
            device_id_type=MESH,
        )

    for k in range(1, n_yz):
        req_copy(k).start()

    link = []
    inverse = []
    for x in range(X):
        b = jnp.broadcast_to(sensor[x : x + 1, :].astype(f32), (ROWS, C))
        alpha = ALPHA_TOP - ALPHA_STEP * b
        den = jnp.ones((ROWS, C), f32) if x == 0 else 1.0 - alpha * link[-1]
        inv = 1.0 / den
        link.append(alpha * inv)
        inverse.append(inv)
        twice = 2.0 * alpha - 1.0
        coef[0, x] = inv * ((193.0 + 126.0 * alpha) / 256.0)
        coef[1, x] = inv * ((105.0 + 302.0 * alpha) / 512.0)
        scaled = inv * twice
        coef[2, x] = scaled * (15.0 / 128.0)
        coef[3, x] = scaled * (-45.0 / 1024.0)
        coef[4, x] = scaled * (5.0 / 512.0)
        coef[5, x] = scaled * (-1.0 / 1024.0)
        coef[6, x] = link[-1]
    y = [-link[0]]
    for x in range(1, X):
        y.append(-link[x] * y[-1])
    ul, ur = (y[-1], -link[-1])
    unit_g[0, X - 1 : X, :] = ul[0:1, :]
    unit_g[1, X - 1 : X, :] = ur[0:1, :]
    ends = [None, ul, None, ur]
    for x in range(X - 2, -1, -1):
        ul = y[x] - link[x] * ul
        ur = -link[x] * ur
        unit_g[0, x : x + 1, :] = ul[0:1, :]
        unit_g[1, x : x + 1, :] = ur[0:1, :]
    ends[0], ends[2] = (ul, ur)
    mine = gains.at[p]
    for i in range(4):
        mine[2 * i : 2 * i + 2, :] = ends[i][0:2, :]

    def gain_copy(k):
        return pltpu.make_async_remote_copy(
            src_ref=gains.at[p],
            dst_ref=gains.at[p],
            send_sem=gain_s.at[k],
            recv_sem=gain_r.at[k],
            device_id=gx(k),
            device_id_type=MESH,
        )

    for k in range(1, n_gx):
        gain_copy(k).start()

    flat = fields[...].reshape(F * X, C)
    for i, piece in enumerate(split3(flat)):
        parts[i * F * X : (i + 1) * F * X, :] = piece

    lane_c = lax.broadcasted_iota(jnp.int32, (C, GP), 0)
    row_x = lax.broadcasted_iota(jnp.int32, (X, GP), 0)
    own = r.astype(f32)

    def rep_copy(k):
        return pltpu.make_async_remote_copy(
            src_ref=answers.at[k // pack],
            dst_ref=reps.at[k],
            send_sem=rep_s.at[k],
            recv_sem=rep_r.at[k],
            device_id=yz(-k),
            device_id_type=MESH,
        )

    for j in range(n_yz // pack):
        block = None
        for i in range(pack):
            k = j * pack + i
            if k:
                req_copy(k).wait_recv()
            piece = reqs[k]
            if i:
                piece = pltpu.roll(piece, i * G, 1)
            block = piece if block is None else block + piece
        hot = jnp.where(lane_c == block[0:1, :].astype(jnp.int32), 1.0, 0.0).astype(bf16)
        got = jnp.dot(parts[...], hot, preferred_element_type=f32)
        offset = row_x - block[1:2, :].astype(jnp.int32)
        mask = jnp.zeros((X, GP), f32)
        for k in range(4):
            mask = jnp.where(offset == k, block[3 + k : 4 + k, :], mask)
        mask = jnp.where(block[2:3, :] == own, mask, 0.0)
        n = F * X
        total = got[0:n] + got[n : 2 * n] + got[2 * n : 3 * n]
        rows = []
        for f in range(F):
            value = jnp.sum(total[f * X : (f + 1) * X] * mask, axis=0, keepdims=True)
            rows.append(SIGNS[f] * value)
        rows.append(jnp.zeros((ROWS - F, GP), f32))
        answers[j] = jnp.concatenate(rows, axis=0)
        for i in range(pack):
            k = j * pack + i
            if k:
                rep_copy(k).start()

    bits = C.bit_length() - 1
    goal = target[...]
    lane = lax.broadcasted_iota(jnp.int32, (1, G), 1)
    goal_x = jnp.right_shift(goal, bits)
    goal_c = jnp.bitwise_and(goal, C - 1)
    wide = lax.broadcasted_iota(jnp.int32, (C, G), 0)
    hit = jnp.where(wide == goal_c, 1.0, 0.0)
    if GP > G:
        hit = jnp.concatenate([hit, jnp.zeros((C, GP - G), f32)], axis=1)
        goal_x = jnp.concatenate([goal_x, jnp.full((1, GP - G), -1, jnp.int32)], axis=1)
    hit = hit.T.astype(bf16)
    for i in range(3):
        onehot_t[i * GP : (i + 1) * GP, :] = hit
    goal_x = jnp.broadcast_to(goal_x, (ROWS, GP))
    ones = jnp.concatenate([jnp.where(goal_x == x, 1.0, 0.0) for x in range(X)], axis=0)
    taken = jnp.dot(ones.astype(bf16), hit, preferred_element_type=f32)
    for x in range(X):
        for f in range(F):
            fb[HALO + x, f : f + 1, :] = fields[f, x : x + 1, :]
    for x in range(X):
        here = taken[x * ROWS : (x + 1) * ROWS]
        fb[HALO + x] = jnp.where(here > 0.5, 0.0, fb[HALO + x])

    link_d, inverse_d, left_d, right_d = thirds_factors(X)
    inter_d = thirds_interface(n_gx, left_d, right_d)
    for x in range(X):
        unit_d[0, x : x + 1, :] = jnp.full((1, C), left_d[x], f32)
        unit_d[1, x : x + 1, :] = jnp.full((1, C), right_d[x], f32)

    inter_g = []
    gain = jnp.zeros((1, C), f32)
    for k in range(1, n_gx):
        gain_from(gains, gain_s, gain_r, k, p, r, n_gx).wait_recv()
    for q in range(n_gx):
        l0, l1 = (gains[q, 0:1, :], gains[q, 2:3, :])
        r0, r1 = (gains[q, 4:5, :], gains[q, 6:7, :])
        s = 1.0 / (1.0 - l0 * gain)
        gf = r0 * s
        ng = r1 + l1 * gain * gf
        inter_g.append((s, l0 * s, gf, l1, l1 * gain, ng))
        gain = ng

    total = answers[0]
    side = None
    for k in range(1, n_yz):
        rep_copy(k).wait_recv()
    sums = [answers[0]] + [None] * (pack - 1)
    for k in range(1, n_yz):
        i = k % pack
        sums[i] = reps[k] if sums[i] is None else sums[i] + reps[k]
    total = sums[0]
    for i in range(1, pack):
        total = total + pltpu.roll(sums[i], GP - i * G, 1)
    stack = []
    for piece in split3(total):
        wide_piece = piece.astype(f32)
        stack.append(
            jnp.concatenate([jnp.where(goal_x == x, wide_piece, 0.0) for x in range(X)], axis=0)
        )
    spread = jnp.dot(
        jnp.concatenate(stack, axis=1).astype(bf16), onehot_t[...], preferred_element_type=f32
    )
    for x in range(X):
        fb[HALO + x] = fb[HALO + x] + spread[x * ROWS : (x + 1) * ROWS]

    def to_above():
        return pltpu.make_async_remote_copy(
            src_ref=fb.at[pl.ds(X, HALO)],
            dst_ref=fb.at[pl.ds(0, HALO)],
            send_sem=halo_s.at[0],
            recv_sem=halo_r.at[0],
            device_id=gx(1),
            device_id_type=MESH,
        )

    def to_below():
        return pltpu.make_async_remote_copy(
            src_ref=fb.at[pl.ds(HALO, HALO)],
            dst_ref=fb.at[pl.ds(HALO + X, HALO)],
            send_sem=halo_s.at[1],
            recv_sem=halo_r.at[1],
            device_id=gx(-1),
            device_id_type=MESH,
        )

    @pl.when(p < n_gx - 1)
    def _():
        to_above().start()

    @pl.when(p > 0)
    def _():
        to_below().start()

    @pl.when(p > 0)
    def _():
        to_above().wait_recv()

    @pl.when(p < n_gx - 1)
    def _():
        to_below().wait_recv()

    yd, yg = ([], [])
    for x in range(X):
        at = HALO + x
        near, next2 = (fb[at + 1], fb[at + 2])
        back, back2 = (fb[at - 1], fb[at - 2])
        slope = (7.0 / 9.0 * inverse_d[x]) * (near - back) + (1.0 / 36.0 * inverse_d[x]) * (
            next2 - back2
        )
        smooth = coef[0, x] * fb[at] + coef[1, x] * (near + back) + coef[2, x] * (next2 + back2)
        for n in range(3, 6):
            smooth = smooth + coef[n, x] * (fb[at + n] + fb[at - n])
        if x:
            slope = slope - link_d[x] * yd[-1]
            smooth = smooth - coef[6, x] * yg[-1]
        yd.append(slope)
        yg.append(smooth)
    ud, ug = (yd[-1], yg[-1])
    last_d, last_g = (ud, ug)
    sol[0, X - 1] = ud
    sol[1, X - 1] = ug
    for x in range(X - 2, -1, -1):
        ud = yd[x] - link_d[x] * ud
        ug = yg[x] - coef[6, x] * ug
        sol[0, x] = ud
        sol[1, x] = ug
    here = edges.at[p]
    for i, v in enumerate((ud, last_d, ug, last_g)):
        here[i * F : (i + 1) * F, :] = v[0:F]

    def edge_copy(k, rank, peer):
        return pltpu.make_async_remote_copy(
            src_ref=edges.at[rank],
            dst_ref=edges.at[rank],
            send_sem=edge_s.at[k],
            recv_sem=edge_r.at[k],
            device_id=peer,
            device_id_type=MESH,
        )

    for k in range(1, n_gx):
        edge_copy(k, p, gx(k)).start()

    for x in range(X):
        for f in range(F):
            out_d[f, x : x + 1, :] = sol[0, x, f : f + 1, :]
            out_g[f, x : x + 1, :] = sol[1, x, f : f + 1, :]

    for k in range(1, n_gx):
        edge_copy(k, lax.rem(p - k + n_gx, n_gx), gx(-k)).wait_recv()

    for which, inter in enumerate((inter_d, inter_g)):
        hold = jnp.zeros((F, C), f32)
        first = []
        pick[which, 0, 0:F, :] = hold
        pick[which, 1, 0:1, :] = jnp.zeros((1, C), f32)
        for q in range(n_gx):
            s, ls, gf, l1, lg, ng = inter[q]
            h0 = edges[q, which * 2 * F : which * 2 * F + F, :]
            h1 = edges[q, which * 2 * F + F : which * 2 * F + 2 * F, :]
            hf = s * h0 + ls * hold
            hold = h1 + l1 * hold + lg * hf
            first.append(hf)
            pick[which, 3 * (q + 1), 0:F, :] = hold
            pick[which, 3 * (q + 1) + 1, 0:1, :] = jnp.broadcast_to(jnp.asarray(ng, f32), (1, C))
        after = jnp.zeros((F, C), f32)
        pick[which, 3 * n_gx + 2, 0:F, :] = after
        for q in range(n_gx - 1, -1, -1):
            after = first[q] + inter[q][2] * after
            pick[which, 3 * q + 2, 0:F, :] = after
        own_first = pick[which, 3 * p + 2, 0:F, :]
        before = pick[which, 3 * p, 0:F, :] + pick[which, 3 * p + 1, 0:1, :] * own_first
        before = jnp.where(p > 0, before, 0.0)
        after = pick[which, 3 * (p + 1) + 2, 0:F, :]
        unit, out = ((unit_d, out_d), (unit_g, out_g))[which]
        lower, upper = (unit[0], unit[1])
        for f in range(F):
            out[f] = out[f] + before[f : f + 1, :] * lower + after[f : f + 1, :] * upper

    for k in range(1, n_yz):
        req_copy(k).wait_send()
        rep_copy(k).wait_send()
    for k in range(1, n_gx):
        gain_copy(k).wait_send()
        edge_copy(k, p, gx(k)).wait_send()

    @pl.when(p < n_gx - 1)
    def _():
        to_above().wait_send()

    @pl.when(p > 0)
    def _():
        to_below().wait_send()


def gain_from(gains, gain_s, gain_r, k, p, r, n_gx):
    rank = lax.rem(p - k + n_gx, n_gx)
    return pltpu.make_async_remote_copy(
        src_ref=gains.at[rank],
        dst_ref=gains.at[rank],
        send_sem=gain_s.at[k],
        recv_sem=gain_r.at[k],
        device_id=(rank, r),
        device_id_type=MESH,
    )


def shards(fields, target, owner, sx, col, weights, sensor):
    F, X, C = fields.shape
    G = target.shape[1]
    n_gx, n_yz = (lax.axis_size("gx"), lax.axis_size("yz"))
    GP = max(G, 128)
    pack = GP // G
    edge_rows = -(-4 * F // ROWS) * ROWS
    f32, bf16 = (jnp.float32, jnp.bfloat16)
    vmem = pl.BlockSpec(memory_space=pltpu.VMEM)
    dma = pltpu.SemaphoreType.DMA
    out = jax.ShapeDtypeStruct(fields.shape, f32)
    return pl.pallas_call(
        functools.partial(kernel, n_gx, n_yz),
        out_shape=(out, out),
        in_specs=[vmem] * 7,
        out_specs=(vmem, vmem),
        scratch_shapes=[
            pltpu.VMEM((3 * F * X, C), bf16),
            pltpu.VMEM((3 * GP, C), bf16),
            pltpu.VMEM((n_yz, ROWS, GP), f32),
            pltpu.VMEM((n_yz, ROWS, GP), f32),
            pltpu.VMEM((n_yz // pack, ROWS, GP), f32),
            pltpu.VMEM((X + 2 * HALO, ROWS, C), f32),
            pltpu.VMEM((7, X, ROWS, C), f32),
            pltpu.VMEM((n_gx, ROWS, C), f32),
            pltpu.VMEM((n_gx, edge_rows, C), f32),
            pltpu.VMEM((2, X, C), f32),
            pltpu.VMEM((2, X, C), f32),
            pltpu.VMEM((2, X, ROWS, C), f32),
            pltpu.VMEM((2, 3 * (n_gx + 1), ROWS, C), f32),
            dma((n_yz,)),
            dma((n_yz,)),
            dma((n_yz,)),
            dma((n_yz,)),
            dma((n_gx,)),
            dma((n_gx,)),
            dma((2,)),
            dma((2,)),
            dma((n_gx,)),
            dma((n_gx,)),
        ],
        compiler_params=pltpu.CompilerParams(collective_id=0, has_side_effects=True),
    )(fields, target, owner.reshape(target.shape), sx, col, weights, sensor)


def solution(mesh):
    placed = (
        P(None, "gx", "yz"),
        P("gx", "yz"),
        P("gx", "yz", None),
        P("gx", "yz"),
        P("gx", "yz"),
        P(None, "gx", "yz"),
        P("gx", "yz"),
    )
    return jax.shard_map(
        shards,
        mesh=mesh,
        in_specs=placed,
        out_specs=(P(None, "gx", "yz"), P(None, "gx", "yz")),
        check_vma=False,
    )
```

time: 641 us -> 24.4 us (0.04); the launches traced: 634 us -> 24.2 us
  other arithmetic: 391 us -> 0 us
  local copies, waits for them, and re-layouts: 204 us -> 2.2 us
  Pallas kernels: 0 us -> 21.4 us
  blocking collectives: 15.4 us -> 0 us
  starting transfers between devices: 14.4 us -> 0 us
    scatter x129 -> x0, other arithmetic: 379 us -> none
    scatter x196 -> x0, local copies, waits for them, and re-layouts: 191 us -> none
    pallas_call x0 -> x1, Pallas kernels: none -> 21.4 us  [shards(): pl.pallas_call(functools.partial(kernel, n_gx, n_yz), out_shape=(out, out...]
    all_gather x1 -> x0, blocking collectives: 15.4 us -> none  [interface_solve(): gathered = lax.all_gather(edges[None], 'gx', axis=0, tiled=True)]
    all_to_all x2 -> x0, starting transfers between devices: 8.55 us -> none  [the longest x1 5.17 us: shards(): lax.all_to_all(payload, 'yz', split_axis=1, concat_axis=1, tiled=True)]
  transfers between devices with their start and end apart: 4 -> 0, of which waited for: 3 -> 0; matrix products, arithmetic and copies ran while one was open for 1% -> 0% of each run, Pallas kernels for 0% -> 0%
where the time goes in v1:
time: 24.4 us; the launch traced here: 24.2 us
  Pallas kernels  21.4 us (88%)
  local copies, waits for them, and re-layouts  2.2 us (9%)
  between operations  0.65 us (3%)
    pallas_call x1, Pallas kernels, shards(): pl.pallas_call(functools.partial(kernel, n_gx, n_yz), out_shape=(out, out...  21.4 us
    unnamed x4, local copies, waits for them, and re-layouts  2.2 us

profile of v1, /device:TPU:0, one launch (start us, length us, event | category | flops | bytes accessed | tf_op | source)
XLA Modules:
  0.0 24.2 jit_solution(15064531753865893096)
XLA Ops:
  0.6 21.4 %shard_map.86 = (f32[5,16,256]{2,1,0:T(8,128)}, f32[5,16,256]{2,1,0:T(8,128)}) custom-call(f32[5,16,256]{2,1,0:T(8,128)} %fields.1, s32[1,64]{1,0:T(1,128)} %target.1, s32[1,64]{1,0:T(1,128)} %bitcast.1, s32[1,64]{1,0:T(1,128)} %sx.1, s32[1,64]{1,0:T(1,128)} %col.1, f32[4,1,64]{2,1,0:T(1,128)} %weights.1, s32[16,256]{1,0:T(8,128)} %sensor.1), custom_call_target="tpu_custom_call" | custom-call | tf_op jit(solution)/shard_map/pallas_call | solution.py:453
  22.0 0.0 copy-start
  22.0 1.6 %copy.11 = f32[5,16,256]{2,1,0:T(8,128)} copy(f32[5,16,256]{2,1,0:T(8,128)} %get-tuple-element.4) | data formatting | bytes 163840
  23.6 0.0 copy-done
  23.6 0.6 %copy.12 = f32[5,16,256]{2,1,0:T(8,128)} copy(f32[5,16,256]{2,1,0:T(8,128)S(1)} %copy-done) | data formatting | bytes 163840
Async XLA Ops:
  22.0 1.6 %copy-start = (f32[5,16,256]{2,1,0:T(8,128)S(1)}, f32[5,16,256]{2,1,0:T(8,128)}, u32[]{:S(2)}) copy-start(f32[5,16,256]{2,1,0:T(8,128)} %get-tuple-element.5) | copy-start | bytes 245764

commit v2 on v1

--- a/solution.py
+++ b/solution.py
@@ -59,6 +59,15 @@
 def kernel(
     n_gx,
     n_yz,
+    fields_hbm,
+    target_hbm,
+    owner_hbm,
+    sx_hbm,
+    col_hbm,
+    weights_hbm,
+    sensor_hbm,
+    out_d,
+    out_g,
     fields,
     target,
     owner,
@@ -66,8 +75,7 @@
     col,
     weights,
     sensor,
-    out_d,
-    out_g,
+    load_sem,
     parts,
     onehot_t,
     reqs,
@@ -107,6 +115,22 @@
         return (lax.rem(p + k + n_gx, n_gx), r)
 
     barrier = pltpu.get_barrier_semaphore()
+    loads = [
+        pltpu.make_async_copy(src, dst, load_sem.at[i])
+        for i, (src, dst) in enumerate(
+            (
+                (owner_hbm, owner),
+                (sx_hbm, sx),
+                (col_hbm, col),
+                (weights_hbm, weights),
+                (sensor_hbm, sensor),
+                (target_hbm, target),
+                (fields_hbm, fields),
+            )
+        )
+    ]
+    for copy in loads:
+        copy.start()
     fb[...] = jnp.zeros_like(fb)
     edges[...] = jnp.zeros_like(edges)
     for k in range(1, n_yz):
@@ -114,6 +138,8 @@
     for k in range(1, n_gx):
         pl.semaphore_signal(barrier, inc=1, device_id=gx(k), device_id_type=MESH)
 
+    for copy in loads[:4]:
+        copy.wait()
     reqs[0] = jnp.zeros((ROWS, GP), f32)
     reqs[0, 0:1, 0:G] = col[...].astype(f32)
     reqs[0, 1:2, 0:G] = sx[...].astype(f32)
@@ -136,6 +162,8 @@
     for k in range(1, n_yz):
         req_copy(k).start()
 
+    for copy in loads[4:]:
+        copy.wait()
     link = []
     inverse = []
     for x in range(X):
@@ -449,13 +477,17 @@
     f32, bf16 = (jnp.float32, jnp.bfloat16)
     vmem = pl.BlockSpec(memory_space=pltpu.VMEM)
     dma = pltpu.SemaphoreType.DMA
-    out = jax.ShapeDtypeStruct(fields.shape, f32)
+    hbm = pl.BlockSpec(memory_space=pltpu.HBM)
+    inputs = (fields, target, target, sx, col, weights, sensor)
+    out = pltpu.VMEM(fields.shape, f32)
     return pl.pallas_call(
         functools.partial(kernel, n_gx, n_yz),
         out_shape=(out, out),
-        in_specs=[vmem] * 7,
+        in_specs=[hbm] * 7,
         out_specs=(vmem, vmem),
         scratch_shapes=[
+            *[pltpu.VMEM(a.shape, a.dtype) for a in inputs],
+            dma((7,)),
             pltpu.VMEM((3 * F * X, C), bf16),
             pltpu.VMEM((3 * GP, C), bf16),
             pltpu.VMEM((n_yz, ROWS, GP), f32),

time: 24.4 us -> 21.9 us (0.90)
  Pallas kernels: 21.4 us -> 19.8 us
  local copies, waits for them, and re-layouts: 2.2 us -> 1.27 us
    pallas_call x1, Pallas kernels: 21.4 us -> 19.8 us  [shards(): pl.pallas_call(functools.partial(kernel, n_gx, n_yz), out_shape=(out, out...]
    unnamed x4 -> x2, local copies, waits for them, and re-layouts: 2.2 us -> 1.27 us
where the time goes in v2:
time: 21.9 us; the launch traced here: 21.7 us
  Pallas kernels  19.8 us (90%)
  local copies, waits for them, and re-layouts  1.27 us (6%)
  between operations  0.64 us (3%)
    pallas_call x1, Pallas kernels, shards(): pl.pallas_call(functools.partial(kernel, n_gx, n_yz), out_shape=(out, out...  19.8 us
    unnamed x2, local copies, waits for them, and re-layouts  1.27 us

profile of v2, /device:TPU:0, one launch (start us, length us, event | category | flops | bytes accessed | tf_op | source)
XLA Modules:
  0.0 21.7 jit_solution(161254982151103225)
XLA Ops:
  0.6 19.8 %shard_map.86 = (f32[5,16,256]{2,1,0:T(8,128)S(1)}, f32[5,16,256]{2,1,0:T(8,128)S(1)}) custom-call(f32[5,16,256]{2,1,0:T(8,128)} %fields_hbm.1, s32[1,64]{1,0:T(1,128)} %target_hbm.1, s32[1,64]{1,0:T(1,128)} %bitcast.1, s32[1,64]{1,0:T(1,128)} %sx_hbm.1, s32[1,64]{1,0:T(1,128)} %col_hbm.1, f32[4,1,64]{2,1,0:T(1,128)} %weights_hbm.1, s32[16,256]{1,0:T(8,128)} %sensor_hbm.1), custom_call_target="tpu_custom_call" | custom-call | tf_op jit(solution)/shard_map/pallas_call | solution.py:483
  20.5 0.6 %copy.11 = f32[5,16,256]{2,1,0:T(8,128)} copy(f32[5,16,256]{2,1,0:T(8,128)S(1)} %get-tuple-element.2) | data formatting | bytes 163840
  21.1 0.6 %copy.12 = f32[5,16,256]{2,1,0:T(8,128)} copy(f32[5,16,256]{2,1,0:T(8,128)S(1)} %get-tuple-element.3) | data formatting | bytes 163840

commit v3 on v2

--- a/solution.py
+++ b/solution.py
@@ -78,6 +78,7 @@
     load_sem,
     parts,
     onehot_t,
+    goals,
     reqs,
     reps,
     answers,
@@ -93,6 +94,8 @@
     req_r,
     rep_s,
     rep_r,
+    goal_s,
+    goal_r,
     gain_s,
     gain_r,
     halo_s,
@@ -123,9 +126,9 @@
                 (sx_hbm, sx),
                 (col_hbm, col),
                 (weights_hbm, weights),
-                (sensor_hbm, sensor),
                 (target_hbm, target),
                 (fields_hbm, fields),
+                (sensor_hbm, sensor),
             )
         )
     ]
@@ -133,6 +136,8 @@
         copy.start()
     fb[...] = jnp.zeros_like(fb)
     edges[...] = jnp.zeros_like(edges)
+    reps[...] = jnp.zeros_like(reps)
+    goals[...] = jnp.full(goals.shape, -1.0, f32)
     for k in range(1, n_yz):
         pl.semaphore_signal(barrier, inc=1, device_id=yz(k), device_id_type=MESH)
     for k in range(1, n_gx):
@@ -162,8 +167,131 @@
     for k in range(1, n_yz):
         req_copy(k).start()
 
-    for copy in loads[4:]:
-        copy.wait()
+    def goal_copy(kind):
+        return pltpu.make_async_remote_copy(
+            src_ref=goals.at[0],
+            dst_ref=goals.at[kind],
+            send_sem=goal_s.at[kind],
+            recv_sem=goal_r.at[kind],
+            device_id=gx(1 if kind == 1 else -1),
+            device_id_type=MESH,
+        )
+
+    def halo_copy(kind):
+        return pltpu.make_async_remote_copy(
+            src_ref=fb.at[pl.ds(X if kind == 1 else HALO, HALO)],
+            dst_ref=fb.at[pl.ds(0 if kind == 1 else HALO + X, HALO)],
+            send_sem=halo_s.at[kind],
+            recv_sem=halo_r.at[kind],
+            device_id=gx(1 if kind == 1 else -1),
+            device_id_type=MESH,
+        )
+
+    has_above = p < n_gx - 1
+    has_below = p > 0
+
+    def each_sent(act):
+        @pl.when(has_above)
+        def _():
+            act(1)
+
+        @pl.when(has_below)
+        def _():
+            act(2)
+
+    def each_received(act):
+        @pl.when(has_below)
+        def _():
+            act(1)
+
+        @pl.when(has_above)
+        def _():
+            act(2)
+
+    bits = C.bit_length() - 1
+    loads[4].wait()
+    goal = target[...]
+    goals[0, 0:1, 0:G] = jnp.right_shift(goal, bits).astype(f32)
+    goals[0, 1:2, 0:G] = jnp.bitwise_and(goal, C - 1).astype(f32)
+    each_sent(lambda kind: goal_copy(kind).start())
+
+    across = lax.broadcasted_iota(jnp.int32, (GP, C), 1).astype(f32)
+
+    def hits(kind):
+        column = jnp.transpose(goals[kind])[:, 1:2]
+        hit = jnp.where(across == column, 1.0, 0.0).astype(bf16)
+        for i in range(3):
+            onehot_t[kind, i * GP : (i + 1) * GP, :] = hit
+        return hit
+
+    loads[5].wait()
+    for x in range(X):
+        for f in range(F):
+            fb[HALO + x, f : f + 1, :] = fields[f, x : x + 1, :]
+    goal_x = jnp.broadcast_to(goals[0, 0:1, :], (ROWS, GP))
+    ones = jnp.concatenate([jnp.where(goal_x == x, 1.0, 0.0) for x in range(X)], axis=0)
+    taken = jnp.dot(ones.astype(bf16), hits(0), preferred_element_type=f32)
+    for x in range(X):
+        here = taken[x * ROWS : (x + 1) * ROWS]
+        fb[HALO + x] = jnp.where(here > 0.5, 0.0, fb[HALO + x])
+    each_sent(lambda kind: halo_copy(kind).start())
+
+    flat = fields[...].reshape(F * X, C)
+    for i, piece in enumerate(split3(flat)):
+        parts[i * F * X : (i + 1) * F * X, :] = piece
+
+    lane_c = lax.broadcasted_iota(jnp.int32, (C, GP), 0)
+    row_x = lax.broadcasted_iota(jnp.int32, (X, GP), 0)
+    own = r.astype(f32)
+
+    def rep_copy(kind, k):
+        rank = lax.rem(p + (0, 1, n_gx - 1)[kind], n_gx)
+        return pltpu.make_async_remote_copy(
+            src_ref=answers.at[k // pack],
+            dst_ref=reps.at[kind, k],
+            send_sem=rep_s.at[kind, k],
+            recv_sem=rep_r.at[kind, k],
+            device_id=(rank, lax.rem(r - k + n_yz, n_yz)),
+            device_id_type=MESH,
+        )
+
+    for j in range(n_yz // pack):
+        block = None
+        for i in range(pack):
+            k = j * pack + i
+            if k:
+                req_copy(k).wait_recv()
+            piece = reqs[k]
+            if i:
+                piece = pltpu.roll(piece, i * G, 1)
+            block = piece if block is None else block + piece
+        hot = jnp.where(lane_c == block[0:1, :].astype(jnp.int32), 1.0, 0.0).astype(bf16)
+        got = jnp.dot(parts[...], hot, preferred_element_type=f32)
+        offset = row_x - block[1:2, :].astype(jnp.int32)
+        mask = jnp.zeros((X, GP), f32)
+        for k in range(4):
+            mask = jnp.where(offset == k, block[3 + k : 4 + k, :], mask)
+        mask = jnp.where(block[2:3, :] == own, mask, 0.0)
+        n = F * X
+        total = got[0:n] + got[n : 2 * n] + got[2 * n : 3 * n]
+        rows = []
+        for f in range(F):
+            value = jnp.sum(total[f * X : (f + 1) * X] * mask, axis=0, keepdims=True)
+            rows.append(SIGNS[f] * value)
+        rows.append(jnp.zeros((ROWS - F, GP), f32))
+        answers[j] = jnp.concatenate(rows, axis=0)
+        for i in range(pack):
+            k = j * pack + i
+            if k:
+                rep_copy(0, k).start()
+
+        def neighbours(kind):
+            for i in range(pack):
+                rep_copy(kind, j * pack + i).start()
+
+        each_sent(neighbours)
+
+    loads[6].wait()
     link = []
     inverse = []
     for x in range(X):
@@ -212,154 +340,53 @@
     for k in range(1, n_gx):
         gain_copy(k).start()
 
-    flat = fields[...].reshape(F * X, C)
-    for i, piece in enumerate(split3(flat)):
-        parts[i * F * X : (i + 1) * F * X, :] = piece
-
-    lane_c = lax.broadcasted_iota(jnp.int32, (C, GP), 0)
-    row_x = lax.broadcasted_iota(jnp.int32, (X, GP), 0)
-    own = r.astype(f32)
-
-    def rep_copy(k):
-        return pltpu.make_async_remote_copy(
-            src_ref=answers.at[k // pack],
-            dst_ref=reps.at[k],
-            send_sem=rep_s.at[k],
-            recv_sem=rep_r.at[k],
-            device_id=yz(-k),
-            device_id_type=MESH,
-        )
-
-    for j in range(n_yz // pack):
-        block = None
-        for i in range(pack):
-            k = j * pack + i
-            if k:
-                req_copy(k).wait_recv()
-            piece = reqs[k]
-            if i:
-                piece = pltpu.roll(piece, i * G, 1)
-            block = piece if block is None else block + piece
-        hot = jnp.where(lane_c == block[0:1, :].astype(jnp.int32), 1.0, 0.0).astype(bf16)
-        got = jnp.dot(parts[...], hot, preferred_element_type=f32)
-        offset = row_x - block[1:2, :].astype(jnp.int32)
-        mask = jnp.zeros((X, GP), f32)
-        for k in range(4):
-            mask = jnp.where(offset == k, block[3 + k : 4 + k, :], mask)
-        mask = jnp.where(block[2:3, :] == own, mask, 0.0)
-        n = F * X
-        total = got[0:n] + got[n : 2 * n] + got[2 * n : 3 * n]
-        rows = []
-        for f in range(F):
-            value = jnp.sum(total[f * X : (f + 1) * X] * mask, axis=0, keepdims=True)
-            rows.append(SIGNS[f] * value)
-        rows.append(jnp.zeros((ROWS - F, GP), f32))
-        answers[j] = jnp.concatenate(rows, axis=0)
-        for i in range(pack):
-            k = j * pack + i
-            if k:
-                rep_copy(k).start()
-
-    bits = C.bit_length() - 1
-    goal = target[...]
-    lane = lax.broadcasted_iota(jnp.int32, (1, G), 1)
-    goal_x = jnp.right_shift(goal, bits)
-    goal_c = jnp.bitwise_and(goal, C - 1)
-    wide = lax.broadcasted_iota(jnp.int32, (C, G), 0)
-    hit = jnp.where(wide == goal_c, 1.0, 0.0)
-    if GP > G:
-        hit = jnp.concatenate([hit, jnp.zeros((C, GP - G), f32)], axis=1)
-        goal_x = jnp.concatenate([goal_x, jnp.full((1, GP - G), -1, jnp.int32)], axis=1)
-    hit = hit.T.astype(bf16)
-    for i in range(3):
-        onehot_t[i * GP : (i + 1) * GP, :] = hit
-    goal_x = jnp.broadcast_to(goal_x, (ROWS, GP))
-    ones = jnp.concatenate([jnp.where(goal_x == x, 1.0, 0.0) for x in range(X)], axis=0)
-    taken = jnp.dot(ones.astype(bf16), hit, preferred_element_type=f32)
-    for x in range(X):
-        for f in range(F):
-            fb[HALO + x, f : f + 1, :] = fields[f, x : x + 1, :]
-    for x in range(X):
-        here = taken[x * ROWS : (x + 1) * ROWS]
-        fb[HALO + x] = jnp.where(here > 0.5, 0.0, fb[HALO + x])
-
     link_d, inverse_d, left_d, right_d = thirds_factors(X)
     inter_d = thirds_interface(n_gx, left_d, right_d)
     for x in range(X):
         unit_d[0, x : x + 1, :] = jnp.full((1, C), left_d[x], f32)
         unit_d[1, x : x + 1, :] = jnp.full((1, C), right_d[x], f32)
 
-    inter_g = []
-    gain = jnp.zeros((1, C), f32)
-    for k in range(1, n_gx):
-        gain_from(gains, gain_s, gain_r, k, p, r, n_gx).wait_recv()
-    for q in range(n_gx):
-        l0, l1 = (gains[q, 0:1, :], gains[q, 2:3, :])
-        r0, r1 = (gains[q, 4:5, :], gains[q, 6:7, :])
-        s = 1.0 / (1.0 - l0 * gain)
-        gf = r0 * s
-        ng = r1 + l1 * gain * gf
-        inter_g.append((s, l0 * s, gf, l1, l1 * gain, ng))
-        gain = ng
-
-    total = answers[0]
-    side = None
+    each_received(lambda kind: goal_copy(kind).wait_recv())
+    hits(1)
+    hits(2)
+
+    each_sent(lambda kind: halo_copy(kind).wait_send())
+    each_received(lambda kind: halo_copy(kind).wait_recv())
     for k in range(1, n_yz):
-        rep_copy(k).wait_recv()
-    sums = [answers[0]] + [None] * (pack - 1)
-    for k in range(1, n_yz):
-        i = k % pack
-        sums[i] = reps[k] if sums[i] is None else sums[i] + reps[k]
-    total = sums[0]
-    for i in range(1, pack):
-        total = total + pltpu.roll(sums[i], GP - i * G, 1)
-    stack = []
-    for piece in split3(total):
-        wide_piece = piece.astype(f32)
-        stack.append(
-            jnp.concatenate([jnp.where(goal_x == x, wide_piece, 0.0) for x in range(X)], axis=0)
-        )
-    spread = jnp.dot(
-        jnp.concatenate(stack, axis=1).astype(bf16), onehot_t[...], preferred_element_type=f32
-    )
-    for x in range(X):
-        fb[HALO + x] = fb[HALO + x] + spread[x * ROWS : (x + 1) * ROWS]
-
-    def to_above():
-        return pltpu.make_async_remote_copy(
-            src_ref=fb.at[pl.ds(X, HALO)],
-            dst_ref=fb.at[pl.ds(0, HALO)],
-            send_sem=halo_s.at[0],
-            recv_sem=halo_r.at[0],
-            device_id=gx(1),
-            device_id_type=MESH,
-        )
-
-    def to_below():
-        return pltpu.make_async_remote_copy(
-            src_ref=fb.at[pl.ds(HALO, HALO)],
-            dst_ref=fb.at[pl.ds(HALO + X, HALO)],
-            send_sem=halo_s.at[1],
-            recv_sem=halo_r.at[1],
-            device_id=gx(-1),
-            device_id_type=MESH,
-        )
-
-    @pl.when(p < n_gx - 1)
-    def _():
-        to_above().start()
-
-    @pl.when(p > 0)
-    def _():
-        to_below().start()
-
-    @pl.when(p > 0)
-    def _():
-        to_above().wait_recv()
-
-    @pl.when(p < n_gx - 1)
-    def _():
-        to_below().wait_recv()
+        rep_copy(0, k).wait_recv()
+
+    def arrived(kind):
+        for k in range(n_yz):
+            rep_copy(kind, k).wait_recv()
+
+    each_received(arrived)
+    for kind, (start, cells) in enumerate(((0, X), (X - HALO, HALO), (0, HALO))):
+        sums = [None] * pack
+        for k in range(n_yz):
+            piece = answers[0] if kind == 0 and k == 0 else reps[kind, k]
+            i = k % pack
+            sums[i] = piece if sums[i] is None else sums[i] + piece
+        total = sums[0]
+        for i in range(1, pack):
+            total = total + pltpu.roll(sums[i], GP - i * G, 1)
+        goal_x = jnp.broadcast_to(goals[kind, 0:1, :], (ROWS, GP))
+        stack = []
+        for piece in split3(total):
+            wide = piece.astype(f32)
+            stack.append(
+                jnp.concatenate(
+                    [jnp.where(goal_x == x, wide, 0.0) for x in range(start, start + cells)],
+                    axis=0,
+                )
+            )
+        spread = jnp.dot(
+            jnp.concatenate(stack, axis=1).astype(bf16),
+            onehot_t[kind],
+            preferred_element_type=f32,
+        )
+        base = (HALO, 0, HALO + X)[kind]
+        for x in range(cells):
+            fb[base + x] = fb[base + x] + spread[x * ROWS : (x + 1) * ROWS]
 
     yd, yg = ([], [])
     for x in range(X):
@@ -407,6 +434,19 @@
         for f in range(F):
             out_d[f, x : x + 1, :] = sol[0, x, f : f + 1, :]
             out_g[f, x : x + 1, :] = sol[1, x, f : f + 1, :]
+
+    inter_g = []
+    gain = jnp.zeros((1, C), f32)
+    for k in range(1, n_gx):
+        gain_from(gains, gain_s, gain_r, k, p, r, n_gx).wait_recv()
+    for q in range(n_gx):
+        l0, l1 = (gains[q, 0:1, :], gains[q, 2:3, :])
+        r0, r1 = (gains[q, 4:5, :], gains[q, 6:7, :])
+        s = 1.0 / (1.0 - l0 * gain)
+        gf = r0 * s
+        ng = r1 + l1 * gain * gf
+        inter_g.append((s, l0 * s, gf, l1, l1 * gain, ng))
+        gain = ng
 
     for k in range(1, n_gx):
         edge_copy(k, lax.rem(p - k + n_gx, n_gx), gx(-k)).wait_recv()
@@ -441,18 +481,17 @@
 
     for k in range(1, n_yz):
         req_copy(k).wait_send()
-        rep_copy(k).wait_send()
+        rep_copy(0, k).wait_send()
     for k in range(1, n_gx):
         gain_copy(k).wait_send()
         edge_copy(k, p, gx(k)).wait_send()
 
-    @pl.when(p < n_gx - 1)
-    def _():
-        to_above().wait_send()
-
-    @pl.when(p > 0)
-    def _():
-        to_below().wait_send()
+    def sent(kind):
+        goal_copy(kind).wait_send()
+        for k in range(n_yz):
+            rep_copy(kind, k).wait_send()
+
+    each_sent(sent)
 
 
 def gain_from(gains, gain_s, gain_r, k, p, r, n_gx):
@@ -489,9 +528,10 @@
             *[pltpu.VMEM(a.shape, a.dtype) for a in inputs],
             dma((7,)),
             pltpu.VMEM((3 * F * X, C), bf16),
-            pltpu.VMEM((3 * GP, C), bf16),
+            pltpu.VMEM((3, 3 * GP, C), bf16),
+            pltpu.VMEM((3, ROWS, GP), f32),
             pltpu.VMEM((n_yz, ROWS, GP), f32),
-            pltpu.VMEM((n_yz, ROWS, GP), f32),
+            pltpu.VMEM((3, n_yz, ROWS, GP), f32),
             pltpu.VMEM((n_yz // pack, ROWS, GP), f32),
             pltpu.VMEM((X + 2 * HALO, ROWS, C), f32),
             pltpu.VMEM((7, X, ROWS, C), f32),
@@ -503,12 +543,14 @@
             pltpu.VMEM((2, 3 * (n_gx + 1), ROWS, C), f32),
             dma((n_yz,)),
             dma((n_yz,)),
-            dma((n_yz,)),
-            dma((n_yz,)),
+            dma((3, n_yz)),
+            dma((3, n_yz)),
+            dma((3,)),
+            dma((3,)),
             dma((n_gx,)),
             dma((n_gx,)),
-            dma((2,)),
-            dma((2,)),
+            dma((3,)),
+            dma((3,)),
             dma((n_gx,)),
             dma((n_gx,)),
         ],

time: 21.9 us -> 20 us (0.913)
  Pallas kernels: 19.8 us -> 17.9 us
    pallas_call x1, Pallas kernels: 19.8 us -> 17.9 us  [shards(): pl.pallas_call(functools.partial(kernel, n_gx, n_yz), out_shape=(out, out...]
where the time goes in v3:
time: 20 us; the launch traced here: 19.8 us
  Pallas kernels  17.9 us (89%)
  local copies, waits for them, and re-layouts  1.27 us (6%)
  between operations  0.64 us (3%)
    pallas_call x1, Pallas kernels, shards(): pl.pallas_call(functools.partial(kernel, n_gx, n_yz), out_shape=(out, out...  17.9 us
    unnamed x2, local copies, waits for them, and re-layouts  1.27 us

profile of v3, /device:TPU:0, one launch (start us, length us, event | category | flops | bytes accessed | tf_op | source)
XLA Modules:
  0.0 19.8 jit_solution(9848786093800809942)
XLA Ops:
  0.6 17.9 %shard_map.86 = (f32[5,16,256]{2,1,0:T(8,128)S(1)}, f32[5,16,256]{2,1,0:T(8,128)S(1)}) custom-call(f32[5,16,256]{2,1,0:T(8,128)} %fields_hbm.1, s32[1,64]{1,0:T(1,128)} %target_hbm.1, s32[1,64]{1,0:T(1,128)} %bitcast.1, s32[1,64]{1,0:T(1,128)} %sx_hbm.1, s32[1,64]{1,0:T(1,128)} %col_hbm.1, f32[4,1,64]{2,1,0:T(1,128)} %weights_hbm.1, s32[16,256]{1,0:T(8,128)} %sensor_hbm.1), custom_call_target="tpu_custom_call" | custom-call | tf_op jit(solution)/shard_map/pallas_call | solution.py:522
  18.5 0.6 %copy.11 = f32[5,16,256]{2,1,0:T(8,128)} copy(f32[5,16,256]{2,1,0:T(8,128)S(1)} %get-tuple-element.2) | data formatting | bytes 163840
  19.2 0.6 %copy.12 = f32[5,16,256]{2,1,0:T(8,128)} copy(f32[5,16,256]{2,1,0:T(8,128)S(1)} %get-tuple-element.3) | data formatting | bytes 163840

commit v4 on v3

--- a/solution.py
+++ b/solution.py
@@ -68,6 +68,8 @@
     sensor_hbm,
     out_d,
     out_g,
+    units,
+    ends,
     fields,
     target,
     owner,
@@ -86,8 +88,6 @@
     coef,
     gains,
     edges,
-    unit_d,
-    unit_g,
     sol,
     pick,
     req_s,
@@ -118,6 +118,10 @@
         return (lax.rem(p + k + n_gx, n_gx), r)
 
     barrier = pltpu.get_barrier_semaphore()
+    for k in range(1, n_yz):
+        pl.semaphore_signal(barrier, inc=1, device_id=yz(k), device_id_type=MESH)
+    for k in range(1, n_gx):
+        pl.semaphore_signal(barrier, inc=1, device_id=gx(k), device_id_type=MESH)
     loads = [
         pltpu.make_async_copy(src, dst, load_sem.at[i])
         for i, (src, dst) in enumerate(
@@ -134,14 +138,22 @@
     ]
     for copy in loads:
         copy.start()
-    fb[...] = jnp.zeros_like(fb)
-    edges[...] = jnp.zeros_like(edges)
-    reps[...] = jnp.zeros_like(reps)
-    goals[...] = jnp.full(goals.shape, -1.0, f32)
-    for k in range(1, n_yz):
-        pl.semaphore_signal(barrier, inc=1, device_id=yz(k), device_id_type=MESH)
-    for k in range(1, n_gx):
-        pl.semaphore_signal(barrier, inc=1, device_id=gx(k), device_id_type=MESH)
+    goals[0] = jnp.full((ROWS, GP), -1.0, f32)
+    for x in range(X):
+        fb[HALO + x] = jnp.zeros((ROWS, C), f32)
+
+    def absent(kind, base):
+        goals[kind] = jnp.full((ROWS, GP), -1.0, f32)
+        fb[base : base + HALO] = jnp.zeros((HALO, ROWS, C), f32)
+        reps[kind] = jnp.zeros((n_yz, ROWS, GP), f32)
+
+    @pl.when(p == 0)
+    def _():
+        absent(1, 0)
+
+    @pl.when(p == n_gx - 1)
+    def _():
+        absent(2, HALO + X)
 
     for copy in loads[:4]:
         copy.wait()
@@ -314,18 +326,18 @@
     for x in range(1, X):
         y.append(-link[x] * y[-1])
     ul, ur = (y[-1], -link[-1])
-    unit_g[0, X - 1 : X, :] = ul[0:1, :]
-    unit_g[1, X - 1 : X, :] = ur[0:1, :]
-    ends = [None, ul, None, ur]
+    units[2, X - 1 : X, :] = ul[0:1, :]
+    units[3, X - 1 : X, :] = ur[0:1, :]
+    tips = [None, ul, None, ur]
     for x in range(X - 2, -1, -1):
         ul = y[x] - link[x] * ul
         ur = -link[x] * ur
-        unit_g[0, x : x + 1, :] = ul[0:1, :]
-        unit_g[1, x : x + 1, :] = ur[0:1, :]
-    ends[0], ends[2] = (ul, ur)
+        units[2, x : x + 1, :] = ul[0:1, :]
+        units[3, x : x + 1, :] = ur[0:1, :]
+    tips[0], tips[2] = (ul, ur)
     mine = gains.at[p]
     for i in range(4):
-        mine[2 * i : 2 * i + 2, :] = ends[i][0:2, :]
+        mine[2 * i : 2 * i + 2, :] = tips[i][0:2, :]
 
     def gain_copy(k):
         return pltpu.make_async_remote_copy(
@@ -343,8 +355,8 @@
     link_d, inverse_d, left_d, right_d = thirds_factors(X)
     inter_d = thirds_interface(n_gx, left_d, right_d)
     for x in range(X):
-        unit_d[0, x : x + 1, :] = jnp.full((1, C), left_d[x], f32)
-        unit_d[1, x : x + 1, :] = jnp.full((1, C), right_d[x], f32)
+        units[0, x : x + 1, :] = jnp.full((1, C), left_d[x], f32)
+        units[1, x : x + 1, :] = jnp.full((1, C), right_d[x], f32)
 
     each_received(lambda kind: goal_copy(kind).wait_recv())
     hits(1)
@@ -414,6 +426,7 @@
         sol[0, x] = ud
         sol[1, x] = ug
     here = edges.at[p]
+    here[...] = jnp.zeros_like(here)
     for i, v in enumerate((ud, last_d, ug, last_g)):
         here[i * F : (i + 1) * F, :] = v[0:F]
 
@@ -474,10 +487,8 @@
         before = pick[which, 3 * p, 0:F, :] + pick[which, 3 * p + 1, 0:1, :] * own_first
         before = jnp.where(p > 0, before, 0.0)
         after = pick[which, 3 * (p + 1) + 2, 0:F, :]
-        unit, out = ((unit_d, out_d), (unit_g, out_g))[which]
-        lower, upper = (unit[0], unit[1])
-        for f in range(F):
-            out[f] = out[f] + before[f : f + 1, :] * lower + after[f : f + 1, :] * upper
+        ends[2 * which] = before
+        ends[2 * which + 1] = after
 
     for k in range(1, n_yz):
         req_copy(k).wait_send()
@@ -519,11 +530,11 @@
     hbm = pl.BlockSpec(memory_space=pltpu.HBM)
     inputs = (fields, target, target, sx, col, weights, sensor)
     out = pltpu.VMEM(fields.shape, f32)
-    return pl.pallas_call(
+    found = pl.pallas_call(
         functools.partial(kernel, n_gx, n_yz),
-        out_shape=(out, out),
+        out_shape=(out, out, pltpu.VMEM((4, X, C), f32), pltpu.VMEM((4, F, C), f32)),
         in_specs=[hbm] * 7,
-        out_specs=(vmem, vmem),
+        out_specs=(vmem, vmem, vmem, vmem),
         scratch_shapes=[
             *[pltpu.VMEM(a.shape, a.dtype) for a in inputs],
             dma((7,)),
@@ -537,8 +548,6 @@
             pltpu.VMEM((7, X, ROWS, C), f32),
             pltpu.VMEM((n_gx, ROWS, C), f32),
             pltpu.VMEM((n_gx, edge_rows, C), f32),
-            pltpu.VMEM((2, X, C), f32),
-            pltpu.VMEM((2, X, C), f32),
             pltpu.VMEM((2, X, ROWS, C), f32),
             pltpu.VMEM((2, 3 * (n_gx + 1), ROWS, C), f32),
             dma((n_yz,)),
@@ -556,6 +565,13 @@
         ],
         compiler_params=pltpu.CompilerParams(collective_id=0, has_side_effects=True),
     )(fields, target, owner.reshape(target.shape), sx, col, weights, sensor)
+    own_d, own_g, units, ends = found
+
+    def whole(local, i):
+        low = ends[2 * i][:, None, :] * units[2 * i][None]
+        return local + low + ends[2 * i + 1][:, None, :] * units[2 * i + 1][None]
+
+    return (whole(own_d, 0), whole(own_g, 1))
 
 
 def solution(mesh):

time: 20 us -> 19.4 us (0.970)
  local copies, waits for them, and re-layouts: 1.27 us -> 0.01 us
  other arithmetic: 0 us -> 0.69 us
    unnamed x2 -> x0, local copies, waits for them, and re-layouts: 1.27 us -> none
    add x0 -> x1, other arithmetic: none -> 0.69 us  [whole(): return local + low + ends[2 * i + 1][:, None, :] * units[2 * i + 1][None]]
where the time goes in v4:
time: 19.4 us; the launch traced here: 19.2 us
  Pallas kernels  17.9 us (92%)
  other arithmetic  0.69 us (4%)
  between operations  0.66 us (3%)
    pallas_call x1, Pallas kernels, shards(): pl.pallas_call(functools.partial(kernel, n_gx, n_yz), out_shape=(out, out...  17.9 us
    add x1, other arithmetic, whole(): return local + low + ends[2 * i + 1][:, None, :] * units[2 * i + 1][None]  0.69 us

profile of v4, /device:TPU:0, one launch (start us, length us, event | category | flops | bytes accessed | tf_op | source)
XLA Modules:
  0.0 19.2 jit_solution(14814026695333966175)
XLA Ops:
  0.6 17.9 %shard_map.86 = (f32[5,16,256]{2,1,0:T(8,128)S(1)}, f32[5,16,256]{2,1,0:T(8,128)S(1)}, f32[4,16,256]{2,1,0:T(8,128)S(1)}, f32[4,5,256]{2,1,0:T(8,128)S(1)}) custom-call(f32[5,16,256]{2,1,0:T(8,128)} %fields_hbm.1, s32[1,64]{1,0:T(1,128)} %target_hbm.1, s32[1,64]{1,0:T(1,128)} %bitcast.17, s32[1,64]{1,0:T(1,128)} %sx_hbm.1, s32[1,64]{1,0:T(1,128)} %col_hbm.1, ...), custom_call_target="tpu_custom_call" | custom-call | tf_op jit(solution)/shard_map/pallas_call | solution.py:533
  18.5 0.7 %multiply_add_fusion = (f32[5,16,256]{2,1,0:T(8,128)}, f32[5,16,256]{2,1,0:T(8,128)}) fusion(f32[5,16,256]{2,1,0:T(8,128)S(1)} %get-tuple-element.9, f32[16,256]{1,0:T(8,128)S(1)} %get-tuple-element.11, f32[5,256]{1,0:T(8,128)S(1)} %get-tuple-element.15, f32[16,256]{1,0:T(8,128)S(1)} %get-tuple-element.10, f32[5,256]{1,0:T(8,128)S(1)} %get-tuple-element.14, ...), kind=kLoop, calls=%fused_computation | loop fusion | flops 163840 | bytes 413696 | tf_op jit(solution)/shard_map/add | solution.py:572
  (2 shorter events, 0.0 us)

commit v5 on v4

--- a/solution.py
+++ b/solution.py
@@ -262,7 +262,7 @@
             src_ref=answers.at[k // pack],
             dst_ref=reps.at[kind, k],
             send_sem=rep_s.at[kind, k],
-            recv_sem=rep_r.at[kind, k],
+            recv_sem=rep_r.at[kind],
             device_id=(rank, lax.rem(r - k + n_yz, n_yz)),
             device_id_type=MESH,
         )
@@ -364,12 +364,19 @@
 
     each_sent(lambda kind: halo_copy(kind).wait_send())
     each_received(lambda kind: halo_copy(kind).wait_recv())
-    for k in range(1, n_yz):
-        rep_copy(0, k).wait_recv()
 
     def arrived(kind):
-        for k in range(n_yz):
-            rep_copy(kind, k).wait_recv()
+        tiles = reps.at[kind, pl.ds(0 if kind else 1, n_yz if kind else n_yz - 1)]
+        pltpu.make_async_remote_copy(
+            src_ref=tiles,
+            dst_ref=tiles,
+            send_sem=rep_s.at[kind, 0],
+            recv_sem=rep_r.at[kind],
+            device_id=yz(1),
+            device_id_type=MESH,
+        ).wait_recv()
+
+    arrived(0)
 
     each_received(arrived)
     for kind, (start, cells) in enumerate(((0, X), (X - HALO, HALO), (0, HALO))):
@@ -460,6 +467,19 @@
         ng = r1 + l1 * gain * gf
         inter_g.append((s, l0 * s, gf, l1, l1 * gain, ng))
         gain = ng
+
+    for k in range(1, n_yz):
+        req_copy(k).wait_send()
+        rep_copy(0, k).wait_send()
+    for k in range(1, n_gx):
+        gain_copy(k).wait_send()
+
+    def sent(kind):
+        goal_copy(kind).wait_send()
+        for k in range(n_yz):
+            rep_copy(kind, k).wait_send()
+
+    each_sent(sent)
 
     for k in range(1, n_gx):
         edge_copy(k, lax.rem(p - k + n_gx, n_gx), gx(-k)).wait_recv()
@@ -490,19 +510,8 @@
         ends[2 * which] = before
         ends[2 * which + 1] = after
 
-    for k in range(1, n_yz):
-        req_copy(k).wait_send()
-        rep_copy(0, k).wait_send()
     for k in range(1, n_gx):
-        gain_copy(k).wait_send()
         edge_copy(k, p, gx(k)).wait_send()
-
-    def sent(kind):
-        goal_copy(kind).wait_send()
-        for k in range(n_yz):
-            rep_copy(kind, k).wait_send()
-
-    each_sent(sent)
 
 
 def gain_from(gains, gain_s, gain_r, k, p, r, n_gx):
@@ -553,7 +562,7 @@
             dma((n_yz,)),
             dma((n_yz,)),
             dma((3, n_yz)),
-            dma((3, n_yz)),
+            dma((3,)),
             dma((3,)),
             dma((3,)),
             dma((n_gx,)),

time: 19.4 us -> 19.1 us (0.985)
  Pallas kernels: 17.9 us -> 17.6 us
    pallas_call x1, Pallas kernels: 17.9 us -> 17.6 us  [shards(): pl.pallas_call(functools.partial(kernel, n_gx, n_yz), out_shape=(out, out...]
where the time goes in v5:
time: 19.1 us; the launch traced here: 19 us
  Pallas kernels  17.6 us (92%)
  other arithmetic  0.69 us (4%)
  between operations  0.66 us (3%)
    pallas_call x1, Pallas kernels, shards(): pl.pallas_call(functools.partial(kernel, n_gx, n_yz), out_shape=(out, out...  17.6 us
    add x1, other arithmetic, whole(): return local + low + ends[2 * i + 1][:, None, :] * units[2 * i + 1][None]  0.69 us

profile of v5, /device:TPU:0, one launch (start us, length us, event | category | flops | bytes accessed | tf_op | source)
XLA Modules:
  0.0 19.0 jit_solution(12840534290567439655)
XLA Ops:
  0.6 17.6 %shard_map.86 = (f32[5,16,256]{2,1,0:T(8,128)S(1)}, f32[5,16,256]{2,1,0:T(8,128)S(1)}, f32[4,16,256]{2,1,0:T(8,128)S(1)}, f32[4,5,256]{2,1,0:T(8,128)S(1)}) custom-call(f32[5,16,256]{2,1,0:T(8,128)} %fields_hbm.1, s32[1,64]{1,0:T(1,128)} %target_hbm.1, s32[1,64]{1,0:T(1,128)} %bitcast.17, s32[1,64]{1,0:T(1,128)} %sx_hbm.1, s32[1,64]{1,0:T(1,128)} %col_hbm.1, ...), custom_call_target="tpu_custom_call" | custom-call | tf_op jit(solution)/shard_map/pallas_call | solution.py:542
  18.3 0.7 %multiply_add_fusion = (f32[5,16,256]{2,1,0:T(8,128)}, f32[5,16,256]{2,1,0:T(8,128)}) fusion(f32[5,16,256]{2,1,0:T(8,128)S(1)} %get-tuple-element.9, f32[16,256]{1,0:T(8,128)S(1)} %get-tuple-element.11, f32[5,256]{1,0:T(8,128)S(1)} %get-tuple-element.15, f32[16,256]{1,0:T(8,128)S(1)} %get-tuple-element.10, f32[5,256]{1,0:T(8,128)S(1)} %get-tuple-element.14, ...), kind=kLoop, calls=%fused_computation | loop fusion | flops 163840 | bytes 413696 | tf_op jit(solution)/shard_map/add | solution.py:581
  (2 shorter events, 0.0 us)
